TPU v7x, 128 devices: a whole 4x4x4 slice. The times are simulated.
128 devices in a mesh: expert: 32 (over z, x, core), etp: 4 (over y).
Axes of the slice: x: 4, y: 4, z: 4, core: 2. Of those that a mesh axis runs over, the one named last changes fastest.
Arguments:
- tokens: bfloat16 [16384, 2560], P(('expert', 'etp')), may hold values from -6 to 6
- routes: int32 [16384, 1], P(('expert', 'etp')), may hold values from 0 to 31; in each aligned block of 128 rows (0 to 127, 128 to 255, ...) at most 12 rows name the same one
- scores: float32 [16384], P(('expert', 'etp')), may hold values from 0.1 to 1
- gate_weight: bfloat16 [32, 2560, 4096], P('expert', None, 'etp'), may hold values from -0.125 to 0.125
- up_weight: bfloat16 [32, 2560, 4096], P('expert', None, 'etp'), may hold values from -0.125 to 0.125
- down_weight: bfloat16 [32, 4096, 2560], P('expert', 'etp'), may hold values from -0.09375 to 0.09375
Outputs:
- layer_out: bfloat16 [16384, 2560], P(('expert', 'etp'))
Inputs may be any that keep to these rules, and one draw needn't show every extreme that they name: `routes`: within each device's aligned block of 128 rows no expert is named by more than 12 rows, a bound that some block reaches; every expert is named by some row.
All inputs are finite; a program needn't handle non-finite values.
Results may differ from a plain program's by a relative error of at most 0.014.
Values may be sent and summed in bfloat16 or wider, within the bound.
A program may use at most 128 MiB of HBM per device.

v0:
```python
import jax
import jax.numpy as jnp
from jax import lax
from jax.sharding import PartitionSpec as P


def hidden_rows(row_block, gate_local, up_local):
    flattened = row_block.reshape(-1, row_block.shape[-1])
    gate_out = jnp.dot(flattened, gate_local, preferred_element_type=jnp.float32)
    up_out = jnp.dot(flattened, up_local, preferred_element_type=jnp.float32)
    hidden = (jax.nn.silu(gate_out) * up_out).astype(jnp.bfloat16)
    return hidden.reshape(row_block.shape[:-1] + (gate_local.shape[1],))


def local(tokens, routes, scores, gate_weight, up_weight, down_weight):
    experts = lax.axis_size("expert")
    groups = lax.axis_size("etp")
    tok_rows, features = tokens.shape
    slot_count = 3 * tok_rows // experts
    expert_ids = routes[:, 0]
    onehot = (expert_ids[:, None] == jnp.arange(experts, dtype=jnp.int32)[None, :]).astype(
        jnp.int32
    )
    position = jnp.sum(
        (jnp.cumsum(onehot, axis=0, dtype=jnp.int32) - 1) * onehot, axis=1, dtype=jnp.int32
    )
    target = expert_ids * slot_count + position
    placing = (
        target[None, :] == jnp.arange(experts * slot_count, dtype=jnp.int32)[:, None]
    ).astype(jnp.bfloat16)
    outgoing = jnp.dot(placing, tokens, preferred_element_type=jnp.float32).astype(jnp.bfloat16)
    outgoing = outgoing.reshape(experts, slot_count, features)
    gate_local = gate_weight[0]
    up_local = up_weight[0]
    down_local = down_weight[0]
    grouped = lax.all_gather(outgoing, "etp", axis=1, tiled=True)
    received = lax.all_to_all(grouped, "expert", split_axis=0, concat_axis=0, tiled=True)
    hidden = hidden_rows(received, gate_local, up_local)
    partial_value = jnp.dot(
        hidden.reshape(-1, hidden.shape[-1]), down_local, preferred_element_type=jnp.float32
    )
    partial_value = partial_value.astype(jnp.bfloat16).reshape(
        experts, groups * slot_count, features
    )
    returned = lax.all_to_all(partial_value, "expert", split_axis=0, concat_axis=0, tiled=True)
    summed = lax.psum_scatter(
        returned.astype(jnp.float32).astype(jnp.bfloat16), "etp", scatter_dimension=1, tiled=True
    )
    collected = lax.dot_general(
        placing,
        summed.reshape(experts * slot_count, features),
        (((0,), (0,)), ((), ())),
        preferred_element_type=jnp.float32,
    )
    return (collected * scores[:, None]).astype(jnp.bfloat16)


def solution(mesh):
    in_specs = (
        P(("expert", "etp"), None),
        P(("expert", "etp"), None),
        P(("expert", "etp")),
        P("expert", None, "etp"),
        P("expert", None, "etp"),
        P("expert", "etp", None),
    )
    out_specs = P(("expert", "etp"), None)
    return jax.shard_map(local, mesh=mesh, in_specs=in_specs, out_specs=out_specs, check_vma=False)
```

profile of v0, /device:TPU:33, one launch (start us, length us, event | category | flops | bytes accessed | tf_op | source)
XLA Modules:
  0.0 434.9 jit_solution(5345934778175982684)
XLA Ops:
  6.5 0.8 fusion.13
  7.3 0.2 reduce_window_sum.11
  7.5 0.8 select_reduce_fusion
  8.3 0.7 multiply_add_fusion
  9.0 1.9 convolution_convert_fusion.1
  11.0 2.5 reshape.21
  13.5 2.5 copy.14
  15.9 0.0 all-gather.2.cloned.1.call-update
  15.9 0.0 reduce-scatter.2.cloned.1.call-start
  16.0 80.9 %all-gather.2.cloned.1.call-done = bf16[32,48,2560]{2,0,1:T(8,128)(2,1)} async-done(((bf16[32,12,2560]{2,0,1:T(8,128)(2,1)}), bf16[32,48,2560]{2,0,1:T(8,128)(2,1)}) %all-gather.2.cloned.1.call-update) | async-done | bytes 7864336 | tf_op jit(solution)/shard_map/all_gather | solution.py:36
  96.9 7.5 %copy.15 = bf16[32,48,2560]{2,1,0:T(8,128)(2,1)S(1)} copy(bf16[32,48,2560]{2,0,1:T(8,128)(2,1)} %all-gather.2.cloned.1.call-done) | data formatting | bytes 15728640 | tf_op jit(solution)/shard_map/all_gather | solution.py:36
  104.4 96.6 %all_to_all.10 = bf16[32,48,2560]{2,1,0:T(8,128)(2,1)S(1)} all-to-all(bf16[32,48,2560]{2,1,0:T(8,128)(2,1)S(1)} %copy.15), channel_id=1, replica_groups=mesh['expert'=32,'etp'=4] {'expert'}, dimensions={0} | all-to-all | bytes 15728640 | tf_op jit(solution)/shard_map/all_to_all | solution.py:37
  201.0 3.1 copy-done.2
  204.1 12.3 %fusion.1 = f32[1536,1024]{1,0:T(8,128)} fusion(bf16[1536,2560]{1,0:T(8,128)(2,1)S(1)} %bitcast.21, bf16[1,2560,1024]{2,1,0:T(8,128)(2,1)} %param.10), kind=kOutput, calls=%fused_computation.3 | convolution fusion | flops 8053063680 | bytes 19398656 | tf_op jit(solution)/shard_map/dot_general | solution.py:10
  216.4 25.3 %convolution_convert_fusion = bf16[1536,2560]{1,0:T(8,128)(2,1)} fusion(bf16[1,1024,2560]{2,1,0:T(8,128)(2,1)} %param.11, f32[1536,1024]{1,0:T(8,128)} %fusion.1, bf16[1536,2560]{1,0:T(8,128)(2,1)} %bitcast.22, bf16[1,2560,1024]{2,1,0:T(8,128)(2,1)} %param.9), kind=kOutput, calls=%fused_computation | convolution fusion | flops 16119496704 | bytes 32505856 | tf_op jit(solution)/shard_map/dot_general | solution.py:39
  241.7 95.1 %all_to_all.11 = bf16[32,48,2560]{2,1,0:T(8,128)(2,1)S(1)} all-to-all(bf16[32,48,2560]{2,1,0:T(8,128)(2,1)} %bitcast.23), channel_id=1, replica_groups=mesh['expert'=32,'etp'=4] {'expert'}, dimensions={0} | all-to-all | bytes 15728640 | tf_op jit(solution)/shard_map/all_to_all | solution.py:45
  336.8 7.4 %copy.16 = bf16[32,48,2560]{2,0,1:T(8,128)(2,1)} copy(bf16[32,48,2560]{2,1,0:T(8,128)(2,1)S(1)} %all_to_all.11) | data formatting | bytes 15728640 | tf_op jit(solution)/shard_map/all_to_all | solution.py:45
  344.2 0.0 reduce-scatter.2.cloned.1.call-update
  344.3 0.0 copy-start.3
  344.3 0.0 copy-start.1
  344.3 76.2 %reduce-scatter.2.cloned.1.call-done = bf16[32,12,2560]{2,0,1:T(8,128)(2,1)} async-done(((bf16[32,48,2560]{2,0,1:T(8,128)(2,1)}), bf16[32,12,2560]{2,0,1:T(8,128)(2,1)}) %reduce-scatter.2.cloned.1.call-update) | async-done | bytes 1966096 | tf_op jit(solution)/shard_map/reduce_scatter | solution.py:46
  420.5 2.7 copy.17
  423.1 2.0 reshape.24
  425.2 2.9 fusion.9
  (6 shorter events, 0.0 us)
Async XLA Ops:
  6.5 2.5 copy-start
  6.5 90.3 %all-gather.2.cloned.1.call-start = ((), (), s32[]{:S(2)}) async-start(), calls=%async_computation.3 | async-start | bytes 9830400 | tf_op jit(solution)/shard_map/all_gather | solution.py:36
  15.9 404.5 %reduce-scatter.2.cloned.1.call-start = ((), (), s32[]{:S(2)}) async-start(), calls=%async_computation.4 | async-start | bytes 9830400 | tf_op jit(solution)/shard_map/reduce_scatter | solution.py:46
  201.0 3.1 copy-start.2
  344.3 80.9 %copy-start.3 = (f32[128]{0:T(128)S(1)}, f32[128]{0:T(128)}, u32[]{:S(2)}) copy-start(f32[128]{0:T(128)} %param.8) | copy-start | bytes 1540
  344.3 83.8 %copy-start.1 = (bf16[128,2560]{1,0:T(8,128)(2,1)S(1)}, bf16[128,2560]{1,0:T(8,128)(2,1)}, u32[]{:S(2)}) copy-start(bf16[128,2560]{1,0:T(8,128)(2,1)} %param.6) | copy-start | bytes 1966084
Sparse Core Ops, SparseCore 0:
  16.1 80.7 all-gather.1
  344.4 76.0 reduce-scatter.1
where the time goes:
time: 437 us; the launch traced here: 435 us
  blocking collectives  192 us (44%)
  waiting for transfers between devices  157 us (36%)
  matrix products  42.5 us (10%)
  local copies, waits for them, and re-layouts  27.6 us (6%)
  between operations  13.5 us (3%)
    all_to_all x1, blocking collectives, local(): lax.all_to_all(grouped, 'expert', split_axis=0, concat_axis=0, tiled=True)  96.6 us
    all_to_all x1, blocking collectives, local(): lax.all_to_all(partial_value, 'expert', split_axis=0, concat_axis=0, tile...  95.1 us
    all_gather x1, waiting for transfers between devices, local(): grouped = lax.all_gather(outgoing, 'etp', axis=1, tiled=True)  80.9 us
    reduce_scatter x1, waiting for transfers between devices, local(): lax.psum_scatter(returned.astype(jnp.float32).astype(jnp.bfloat16), 'etp'...  76.2 us
    dot_general x1, matrix products, local(): jnp.dot(hidden.reshape(-1, hidden.shape[-1]), down_local, preferred_eleme...  25.3 us
    dot_general x1, matrix products, hidden_rows(): up_out = jnp.dot(flattened, up_local, preferred_element_type=jnp.float32)  12.3 us
  transfers between devices with their start and end apart: 2, of which 2 were waited for; matrix products, arithmetic and copies ran while one was open for 0% of the time, Pallas kernels for 0%

commit v1 on v0

--- a/solution.py
+++ b/solution.py
@@ -14,16 +14,12 @@
 
 def local(tokens, routes, scores, gate_weight, up_weight, down_weight):
     experts = lax.axis_size("expert")
-    groups = lax.axis_size("etp")
     tok_rows, features = tokens.shape
     slot_count = 3 * tok_rows // experts
     expert_ids = routes[:, 0]
-    onehot = (expert_ids[:, None] == jnp.arange(experts, dtype=jnp.int32)[None, :]).astype(
-        jnp.int32
-    )
-    position = jnp.sum(
-        (jnp.cumsum(onehot, axis=0, dtype=jnp.int32) - 1) * onehot, axis=1, dtype=jnp.int32
-    )
+    earlier = jnp.arange(tok_rows)[:, None] < jnp.arange(tok_rows)[None, :]
+    same = expert_ids[:, None] == expert_ids[None, :]
+    position = jnp.sum((same & earlier).astype(jnp.int32), axis=0, dtype=jnp.int32)
     target = expert_ids * slot_count + position
     placing = (
         target[None, :] == jnp.arange(experts * slot_count, dtype=jnp.int32)[:, None]
@@ -33,18 +29,20 @@
     gate_local = gate_weight[0]
     up_local = up_weight[0]
     down_local = down_weight[0]
-    grouped = lax.all_gather(outgoing, "etp", axis=1, tiled=True)
-    received = lax.all_to_all(grouped, "expert", split_axis=0, concat_axis=0, tiled=True)
-    hidden = hidden_rows(received, gate_local, up_local)
-    partial_value = jnp.dot(
-        hidden.reshape(-1, hidden.shape[-1]), down_local, preferred_element_type=jnp.float32
+    received = lax.all_to_all(outgoing, "expert", split_axis=0, concat_axis=0, tiled=True)
+    grouped = lax.all_gather(
+        received.reshape(experts * slot_count, features), "etp", axis=0, tiled=True
     )
-    partial_value = partial_value.astype(jnp.bfloat16).reshape(
-        experts, groups * slot_count, features
-    )
-    returned = lax.all_to_all(partial_value, "expert", split_axis=0, concat_axis=0, tiled=True)
-    summed = lax.psum_scatter(
-        returned.astype(jnp.float32).astype(jnp.bfloat16), "etp", scatter_dimension=1, tiled=True
+    hidden = hidden_rows(grouped, gate_local, up_local)
+    partial_value = jnp.dot(hidden, down_local, preferred_element_type=jnp.float32)
+    partial_value = partial_value.astype(jnp.bfloat16)
+    summed = lax.psum_scatter(partial_value, "etp", scatter_dimension=0, tiled=True)
+    summed = lax.all_to_all(
+        summed.reshape(experts, slot_count, features),
+        "expert",
+        split_axis=0,
+        concat_axis=0,
+        tiled=True,
     )
     collected = lax.dot_general(
         placing,

time: 437 us -> 309 us (0.71)
  blocking collectives: 192 us -> 81.5 us
  local copies, waits for them, and re-layouts: 27.6 us -> 11.7 us
    all_to_all x2, blocking collectives: 192 us -> 81.5 us  [the longest x1 41.1 us: local(): lax.all_to_all(outgoing, 'expert', split_axis=0, concat_axis=0, tiled=True)]
    all_gather x1 -> x0, local copies, waits for them, and re-layouts: 7.54 us -> none  [local(): grouped = lax.all_gather(outgoing, 'etp', axis=1, tiled=True)]
    all_to_all x1 -> x0, local copies, waits for them, and re-layouts: 7.39 us -> none  [local(): lax.all_to_all(partial_value, 'expert', split_axis=0, concat_axis=0, tile...]
    reshape x0 -> x2, local copies, waits for them, and re-layouts: none -> 6.52 us  [the longest x1 4.04 us: local(): received.reshape(experts * slot_count, features)]
where the time goes in v1:
time: 309 us; the launch traced here: 306 us
  waiting for transfers between devices  155 us (50%)
  blocking collectives  81.5 us (26%)
  matrix products  42.5 us (14%)
  between operations  13.4 us (4%)
  local copies, waits for them, and re-layouts  11.7 us (4%)
    reduce_scatter x1, waiting for transfers between devices, local(): lax.psum_scatter(partial_value, 'etp', scatter_dimension=0, tiled=True)  77.9 us
    all_gather x1, waiting for transfers between devices, local(): lax.all_gather(received.reshape(experts * slot_count, features), 'etp', a...  77.5 us
    all_to_all x1, blocking collectives, local(): lax.all_to_all(outgoing, 'expert', split_axis=0, concat_axis=0, tiled=True)  41.1 us
    all_to_all x1, blocking collectives, local(): lax.all_to_all(summed.reshape(experts, slot_count, features), 'expert', s...  40.5 us
    dot_general x1, matrix products, local(): jnp.dot(hidden, down_local, preferred_element_type=jnp.float32)  25.3 us
    dot_general x1, matrix products, hidden_rows(): up_out = jnp.dot(flattened, up_local, preferred_element_type=jnp.float32)  13.8 us
  transfers between devices with their start and end apart: 2, of which 2 were waited for; matrix products, arithmetic and copies ran while one was open for 0% of the time, Pallas kernels for 0%

profile of v1, /device:TPU:33, one launch (start us, length us, event | category | flops | bytes accessed | tf_op | source)
XLA Modules:
  0.0 306.1 jit_solution(9060369646275938181)
XLA Ops:
  6.5 0.0 copy-start
  6.5 0.0 all-gather.2.cloned.1.call-start
  6.5 0.8 convert_reduce_fusion
  7.4 0.7 multiply_add_fusion
  8.0 0.0 copy-done
  8.0 2.0 convolution_convert_fusion.1
  10.0 2.5 reshape.22
  12.5 41.1 %all_to_all.10 = bf16[32,12,2560]{2,1,0:T(8,128)(2,1)} all-to-all(bf16[32,12,2560]{2,1,0:T(8,128)(2,1)S(1)} %reshape.22), channel_id=1, replica_groups=mesh['expert'=32,'etp'=4] {'expert'}, dimensions={0} | all-to-all | bytes 3932160 | tf_op jit(solution)/shard_map/all_to_all | solution.py:32
  53.6 4.0 %reshape.23 = bf16[384,2560]{1,0:T(8,128)(2,1)} reshape(bf16[32,12,2560]{2,1,0:T(8,128)(2,1)} %all_to_all.10) | data formatting | bytes 3932160 | tf_op jit(solution)/shard_map/reshape | solution.py:34
  57.6 0.0 all-gather.2.cloned.1.call-update
  57.6 0.0 reduce-scatter.2.cloned.1.call-start
  57.7 77.5 %all-gather.2.cloned.1.call-done = bf16[1536,2560]{1,0:T(8,128)(2,1)} async-done(((bf16[384,2560]{1,0:T(8,128)(2,1)}), bf16[1536,2560]{1,0:T(8,128)(2,1)}) %all-gather.2.cloned.1.call-update) | async-done | bytes 7864336 | tf_op jit(solution)/shard_map/all_gather | solution.py:33
  135.2 13.8 %fusion.1 = f32[1536,1024]{1,0:T(8,128)} fusion(bf16[1536,2560]{1,0:T(8,128)(2,1)} %all-gather.2.cloned.1.call-done, bf16[1,2560,1024]{2,1,0:T(8,128)(2,1)} %param.10), kind=kOutput, calls=%fused_computation.3 | convolution fusion | flops 8053063680 | bytes 19398656 | tf_op jit(solution)/shard_map/dot_general | solution.py:10
  149.0 25.3 %convolution_convert_fusion = bf16[1536,2560]{1,0:T(8,128)(2,1)} fusion(bf16[1,1024,2560]{2,1,0:T(8,128)(2,1)} %param.11, f32[1536,1024]{1,0:T(8,128)} %fusion.1, bf16[1536,2560]{1,0:T(8,128)(2,1)} %all-gather.2.cloned.1.call-done, bf16[1,2560,1024]{2,1,0:T(8,128)(2,1)} %param.9), kind=kOutput, calls=%fused_computation | convolution fusion | flops 16119496704 | bytes 32505856 | tf_op jit(solution)/shard_map/dot_general | solution.py:37
  174.3 0.0 reduce-scatter.2.cloned.1.call-update
  174.3 77.9 %reduce-scatter.2.cloned.1.call-done = bf16[384,2560]{1,0:T(8,128)(2,1)} async-done(((bf16[1536,2560]{1,0:T(8,128)(2,1)}), bf16[384,2560]{1,0:T(8,128)(2,1)}) %reduce-scatter.2.cloned.1.call-update) | async-done | bytes 1966096 | tf_op jit(solution)/shard_map/reduce_scatter | solution.py:39
  252.3 2.5 reshape.24
  254.7 0.0 copy-start.1
  254.8 40.5 %all_to_all.11 = bf16[32,12,2560]{2,1,0:T(8,128)(2,1)} all-to-all(bf16[32,12,2560]{2,1,0:T(8,128)(2,1)S(1)} %reshape.24), channel_id=1, replica_groups=mesh['expert'=32,'etp'=4] {'expert'}, dimensions={0} | all-to-all | bytes 3932160 | tf_op jit(solution)/shard_map/all_to_all | solution.py:40
  295.2 2.7 reshape.25
  297.9 0.0 copy-done.1
  297.9 1.4 fusion.9
Async XLA Ops:
  6.5 1.5 copy-start
  6.5 128.7 %all-gather.2.cloned.1.call-start = ((), (), s32[]{:S(2)}) async-start(), calls=%async_computation.3 | async-start | bytes 9830400 | tf_op jit(solution)/shard_map/all_gather | solution.py:33
  57.6 194.6 %reduce-scatter.2.cloned.1.call-start = ((), (), s32[]{:S(2)}) async-start(), calls=%async_computation.4 | async-start | bytes 9830400 | tf_op jit(solution)/shard_map/reduce_scatter | solution.py:39
  254.7 43.1 %copy-start.1 = (f32[128]{0:T(128)S(1)}, f32[128]{0:T(128)}, u32[]{:S(2)}) copy-start(f32[128]{0:T(128)} %param.8) | copy-start | bytes 1540
Sparse Core Ops, SparseCore 0:
  57.7 77.4 all-gather.1
  174.4 77.7 reduce-scatter.1

commit v2 on v1

v2 whole, which is shorter than its diff:
```python
import jax
import jax.numpy as jnp
from jax import lax
from jax.experimental import pallas as pl
from jax.experimental.pallas import tpu as pltpu
from jax.sharding import PartitionSpec as P

MESH = pl.DeviceIdType.MESH
CAP = 12
ORDER = (0, 1, 3, 2)


def layer(
    tokens,
    routes_row,
    routes_col,
    scores,
    gate_hbm,
    up_hbm,
    down_hbm,
    out,
    gate,
    up,
    down,
    codes,
    partner_codes,
    partner_tokens,
    place,
    outgoing,
    rows_in,
    lhs,
    hidden,
    partials,
    far,
    near,
    returned,
    cross_out,
    cross_in,
    weight_sem,
    pair_s,
    pair_r,
    zx_s,
    zx_r,
    hop1_s,
    hop1_r,
    hop2_s,
    hop2_r,
    far_s,
    far_r,
    near_s,
    near_r,
    back_s,
    back_r,
):
    e, y = lax.axis_index("expert"), lax.axis_index("etp")
    core, x, z = e % 2, (e // 2) % 4, e // 8
    features = tokens.shape[1]
    chunk_rows = lhs.shape[0]
    partner = (e + 1 - 2 * core, y)
    ups, downs = (e, (y + 1) % 4), (e, (y + 3) % 4)

    def owner(dz, dx):
        return ((((z + dz) % 4) * 4 + (x + dx) % 4) * 2 + core, y)

    def remote(src, dst, send, recv, to):
        return pltpu.make_async_remote_copy(
            src_ref=src, dst_ref=dst, send_sem=send, recv_sem=recv, device_id=to, device_id_type=MESH
        )

    weights = [
        pltpu.make_async_copy(gate_hbm, gate, weight_sem.at[0]),
        pltpu.make_async_copy(up_hbm, up, weight_sem.at[1]),
        pltpu.make_async_copy(down_hbm, down, weight_sem.at[2]),
    ]

    swap_tokens = remote(tokens, partner_tokens, pair_s.at[0], pair_r.at[0], partner)
    swap_tokens.start()
    for w in weights:
        w.start()
    tok = tokens.shape[0]
    row = routes_row[...]
    col = routes_col[...]
    first = lax.broadcasted_iota(jnp.int32, (tok, tok), 0)
    second = lax.broadcasted_iota(jnp.int32, (tok, tok), 1)
    same = col == row

    def code_of(route, position):
        chip = ((route // 8 - z) & 3) * 4 + ((route // 2 - x) & 3)
        return (route & 1) * 1024 + chip * (2 * CAP) + core * CAP + position

    pos_row = jnp.sum(jnp.where(same & (first < second), 1.0, 0.0), axis=0, keepdims=True)
    pos_col = jnp.sum(jnp.where(same & (second < first), 1.0, 0.0), axis=1, keepdims=True)
    codes[0:tok, :] = jnp.broadcast_to(code_of(col, pos_col.astype(jnp.int32)), (tok, tok))
    codes[tok : tok + 8, :] = jnp.broadcast_to(code_of(row, pos_row.astype(jnp.int32)), (8, tok))
    swap_codes = remote(codes, partner_codes, pair_s.at[1], pair_r.at[1], partner)
    swap_codes.start()
    slots = place.shape[0]
    slot = lax.broadcasted_iota(jnp.int32, (slots, tok), 0)

    def marks(code):
        return jnp.where(slot == code - core * 1024, 1.0, 0.0).astype(jnp.bfloat16)

    place[:, 0:tok] = marks(codes[tok : tok + 1, :])
    swap_codes.wait_recv()
    place[:, tok : 2 * tok] = marks(partner_codes[tok : tok + 1, :])
    swap_tokens.wait_recv()

    def send_zx(dz, dx):
        o = (4 - dz) % 4
        s = (4 - dx) % 4
        return remote(
            outgoing.at[dz, pl.ds(3 * dx, 3)],
            rows_in.at[o, 0, pl.ds(3 * s, 3)],
            zx_s.at[dz * 4 + dx],
            zx_r.at[o * 4 + s],
            owner(dz, dx),
        )

    def hop1(o, up_way, half):
        part = pl.ds(6 * half, 6)
        k = o * 4 + up_way * 2 + half
        return remote(
            rows_in.at[o, 0, part],
            rows_in.at[o, 3 if up_way else 1, part],
            hop1_s.at[k],
            hop1_r.at[k],
            ups if up_way else downs,
        )

    def hop2(o, up_way):
        part = pl.ds(0 if up_way else 6, 6)
        k = o * 2 + up_way
        return remote(
            rows_in.at[o, 3 if up_way else 1, part],
            rows_in.at[o, 2, part],
            hop2_s.at[k],
            hop2_r.at[k],
            ups if up_way else downs,
        )

    def send_far(o, up_way):
        k = o * 2 + up_way
        return remote(
            partials.at[o, 2, pl.ds(0 if up_way else 6, 6)],
            far.at[o, up_way],
            far_s.at[k],
            far_r.at[k],
            ups if up_way else downs,
        )

    def send_near(o, up_way, half):
        part = pl.ds(6 * half, 6)
        k = o * 4 + up_way * 2 + half
        return remote(
            partials.at[o, 1 if up_way else 3, part],
            near.at[o, up_way, part],
            near_s.at[k],
            near_r.at[k],
            ups if up_way else downs,
        )

    def send_back(o, dx):
        v, s = (4 - o) % 4, (4 - dx) % 4
        return remote(
            partials.at[o, 0, pl.ds(3 * dx, 3)],
            returned.at[v, pl.ds(3 * s, 3)],
            back_s.at[o * 4 + dx],
            back_r.at[v * 4 + s],
            owner(o, dx),
        )

    group = slots // 4
    for o in ORDER:
        dz = (4 - o) % 4

        @pl.loop(0, features // 256)
        def _(n):
            cols = pl.ds(pl.multiple_of(n * 256, 256), 256)
            mark = place[dz * group : (dz + 1) * group, :]
            got = jnp.dot(mark[:, 0:tok], tokens[:, cols], preferred_element_type=jnp.float32)
            got += jnp.dot(mark[:, tok:], partner_tokens[:, cols], preferred_element_type=jnp.float32)
            outgoing[dz, :, :, cols] = got.astype(jnp.bfloat16).reshape(group // 8, 8, 256)

        for dx in range(4):
            if dz or dx:
                send_zx(dz, dx).start()
            else:
                rows_in[0, 0, 0:3] = outgoing[0, 0:3]

    def start_hop1(o):
        for s in range(4):
            if o or s:
                send_zx((4 - o) % 4, (4 - s) % 4).wait_recv()
        hop1(o, 1, 0).start()
        hop1(o, 0, 1).start()
        hop1(o, 1, 1).start()
        hop1(o, 0, 0).start()

    def start_hop2(o):
        hop1(o, 1, 0).wait_recv()
        hop2(o, 1).start()
        hop1(o, 0, 1).wait_recv()
        hop2(o, 0).start()

    def compute(o):
        hop1(o, 1, 1).wait_recv()
        hop1(o, 0, 0).wait_recv()
        hop2(o, 1).wait_recv()
        hop2(o, 0).wait_recv()
        part_rows = chunk_rows // 4
        for k in range(4):
            lhs[k * part_rows : (k + 1) * part_rows, :] = rows_in[o, k].reshape(part_rows, features)

        @pl.loop(0, hidden.shape[1] // 256)
        def _(n):
            cols = pl.ds(pl.multiple_of(n * 256, 256), 256)
            g = jnp.dot(lhs[...], gate[:, cols], preferred_element_type=jnp.float32)
            u = jnp.dot(lhs[...], up[:, cols], preferred_element_type=jnp.float32)
            hidden[:, cols] = (g / (1.0 + jnp.exp(-g)) * u).astype(jnp.bfloat16)

        @pl.loop(0, features // 256)
        def _(n):
            cols = pl.ds(pl.multiple_of(n * 256, 256), 256)
            p = jnp.dot(hidden[...], down[:, cols], preferred_element_type=jnp.float32)
            partials[o, :, :, :, cols] = p.astype(jnp.bfloat16).reshape(4, part_rows // 8, 8, 256)

        send_far(o, 1).start()
        send_far(o, 0).start()
        send_near(o, 1, 1).start()
        send_near(o, 0, 0).start()

    def add_far(o):
        for up_way in (1, 0):
            half = 0 if up_way else 1
            part = pl.ds(6 * half, 6)
            send_far(o, up_way).wait_recv()
            k = 1 if up_way else 3
            partials[o, k, part] = (
                partials[o, k, part].astype(jnp.float32) + far[o, up_way].astype(jnp.float32)
            ).astype(jnp.bfloat16)
            send_near(o, up_way, half).start()

    def finish(o):
        for up_way in (0, 1):
            for half in (0, 1):
                send_near(o, up_way, half).wait_recv()
        for dx in range(4):
            part = pl.ds(3 * dx, 3)
            total = (
                partials[o, 0, part].astype(jnp.float32)
                + near[o, 0, part].astype(jnp.float32)
                + near[o, 1, part].astype(jnp.float32)
            ).astype(jnp.bfloat16)
            if o or dx:
                partials[o, 0, part] = total
                send_back(o, dx).start()
            else:
                returned[0, 0:3] = total

    start_hop1(ORDER[0])
    start_hop2(ORDER[0])
    start_hop1(ORDER[1])
    for w in weights:
        w.wait()
    for i, o in enumerate(ORDER):
        compute(o)
        if i + 1 < 4:
            start_hop2(ORDER[i + 1])
        if i + 2 < 4:
            start_hop1(ORDER[i + 2])
        if i >= 1:
            add_far(ORDER[i - 1])
        if i >= 2:
            finish(ORDER[i - 2])
    add_far(ORDER[3])
    finish(ORDER[2])
    finish(ORDER[3])

    for v in range(4):
        for s in range(4):
            if v or s:
                send_back((4 - v) % 4, (4 - s) % 4).wait_recv()
    for v in range(4):
        lhs[v * group : (v + 1) * group, :] = returned[v].reshape(group, features)
    slot_lane = lax.broadcasted_iota(jnp.int32, (tok, slots), 1)

    def picks(code):
        return jnp.where(slot_lane == code - core * 1024, 1.0, 0.0).astype(jnp.bfloat16)

    theirs, ours = picks(partner_codes[0:tok, 0:1]), picks(codes[0:tok, 0:1])
    cross_out[...] = jnp.dot(theirs, lhs[...], preferred_element_type=jnp.float32).astype(jnp.bfloat16)
    swap_back = remote(cross_out, cross_in, pair_s.at[2], pair_r.at[2], partner)
    swap_back.start()
    mine = jnp.dot(ours, lhs[...], preferred_element_type=jnp.float32)
    swap_back.wait_recv()
    out[...] = (scores[...] * (mine + cross_in[...].astype(jnp.float32))).astype(jnp.bfloat16)

    swap_tokens.wait_send()
    swap_codes.wait_send()
    swap_back.wait_send()
    for a in range(4):
        for b in range(4):
            if a or b:
                send_zx(a, b).wait_send()
                send_back(a, b).wait_send()
        for way in (0, 1):
            hop2(a, way).wait_send()
            send_far(a, way).wait_send()
            for half in (0, 1):
                hop1(a, way, half).wait_send()
                send_near(a, way, half).wait_send()


def local(tokens, routes, scores, gate_weight, up_weight, down_weight):
    tok, features = tokens.shape
    hid = gate_weight.shape[2]
    slots = 32 * CAP
    group = slots // 4
    bf = jnp.bfloat16
    vmem = pl.BlockSpec(memory_space=pltpu.VMEM)
    hbm = pl.BlockSpec(memory_space=pl.ANY)
    dma = pltpu.SemaphoreType.DMA
    return pl.pallas_call(
        layer,
        out_shape=jax.ShapeDtypeStruct((tok, features), bf),
        in_specs=[vmem] * 4 + [hbm] * 3,
        out_specs=vmem,
        scratch_shapes=[
            pltpu.VMEM((features, hid), bf),
            pltpu.VMEM((features, hid), bf),
            pltpu.VMEM((hid, features), bf),
            pltpu.VMEM((tok + 8, tok), jnp.int32),
            pltpu.VMEM((tok + 8, tok), jnp.int32),
            pltpu.VMEM((tok, features), bf),
            pltpu.VMEM((slots, 2 * tok), bf),
            pltpu.VMEM((4, group // 8, 8, features), bf),
            pltpu.VMEM((4, 4, group // 8, 8, features), bf),
            pltpu.VMEM((slots, features), bf),
            pltpu.VMEM((slots, hid), bf),
            pltpu.VMEM((4, 4, group // 8, 8, features), bf),
            pltpu.VMEM((4, 2, group // 16, 8, features), bf),
            pltpu.VMEM((4, 2, group // 8, 8, features), bf),
            pltpu.VMEM((4, group // 8, 8, features), bf),
            pltpu.VMEM((tok, features), bf),
            pltpu.VMEM((tok, features), bf),
            dma((3,)),
            dma((3,)),
            dma((3,)),
            dma((16,)),
            dma((16,)),
            dma((16,)),
            dma((16,)),
            dma((8,)),
            dma((8,)),
            dma((8,)),
            dma((8,)),
            dma((16,)),
            dma((16,)),
            dma((16,)),
            dma((16,)),
        ],
        compiler_params=pltpu.CompilerParams(
            has_side_effects=True, vmem_limit_bytes=62 * 1024 * 1024
        ),
    )(
        tokens,
        routes.reshape(1, tok),
        routes,
        scores.reshape(tok, 1),
        gate_weight[0],
        up_weight[0],
        down_weight[0],
    )


def solution(mesh):
    in_specs = (
        P(("expert", "etp"), None),
        P(("expert", "etp"), None),
        P(("expert", "etp")),
        P("expert", None, "etp"),
        P("expert", None, "etp"),
        P("expert", "etp", None),
    )
    out_specs = P(("expert", "etp"), None)
    return jax.shard_map(local, mesh=mesh, in_specs=in_specs, out_specs=out_specs, check_vma=False)
```

time: 309 us -> 179 us (0.58)
  Pallas kernels: 0 us -> 174 us
  waiting for transfers between devices: 155 us -> 0 us
  blocking collectives: 81.5 us -> 0 us
  matrix products: 42.5 us -> 0 us
  between operations: 13.4 us -> 0.01 us
  local copies, waits for them, and re-layouts: 11.7 us -> 4.73 us
    pallas_call x0 -> x1, Pallas kernels: none -> 174 us  [local(): pl.pallas_call(layer, out_shape=jax.ShapeDtypeStruct((tok, features), bf)...]
    all_to_all x2 -> x0, blocking collectives: 81.5 us -> none  [the longest x1 41.1 us: local(): lax.all_to_all(outgoing, 'expert', split_axis=0, concat_axis=0, tiled=True)]
    reduce_scatter x1 -> x0, waiting for transfers between devices: 77.9 us -> none  [local(): lax.psum_scatter(partial_value, 'etp', scatter_dimension=0, tiled=True)]
    all_gather x1 -> x0, waiting for transfers between devices: 77.5 us -> none  [local(): lax.all_gather(received.reshape(experts * slot_count, features), 'etp', a...]
    dot_general x4 -> x0, matrix products: 42.5 us -> none  [the longest x1 25.3 us: local(): jnp.dot(hidden, down_local, preferred_element_type=jnp.float32)]
    reshape x4 -> x1, local copies, waits for them, and re-layouts: 11.6 us -> 1.38 us  [local(): scores.reshape(tok, 1)]
    unnamed x4 -> x2, local copies, waits for them, and re-layouts: 0.01 us -> 3.36 us
  transfers between devices with their start and end apart: 2 -> 0, of which waited for: 2 -> 0; matrix products, arithmetic and copies ran while one was open for 0% -> 0% of each run, Pallas kernels for 0% -> 0%
where the time goes in v2:
time: 179 us
  Pallas kernels  174 us (97%)
  local copies, waits for them, and re-layouts  4.73 us (3%)
    pallas_call x1, Pallas kernels, local(): pl.pallas_call(layer, out_shape=jax.ShapeDtypeStruct((tok, features), bf)...  174 us

profile of v2, /device:TPU:33, one launch (start us, length us, event | category | flops | bytes accessed | tf_op | source)
XLA Modules:
  0.0 178.8 jit_solution(5191955501277667526)
XLA Ops:
  0.0 1.4 copy.8.scores
  1.4 1.4 copy.7.routes_col
  2.8 174.1 %shard_map.64 = bf16[128,2560]{1,0:T(8,128)(2,1)} custom-call(bf16[128,2560]{1,0:T(8,128)(2,1)} %tokens.1, s32[1,128]{1,0:T(1,128)} %bitcast.8, s32[128,1]{1,0:T(8,128)} %copy.7.routes_col, f32[128,1]{1,0:T(8,128)} %copy.8.scores, bf16[2560,1024]{1,0:T(8,128)(2,1)} %bitcast.5, bf16[2560,1024]{1,0:T(8,128)(2,1)} %bitcast.6, bf16[1024,2560]{1,0:T(8,128)(2,1)} %bitcast.7), custom_call_target="tpu_custom_call" | custom-call | tf_op jit(solution)/shard_map/pallas_call | solution.py:323
  176.8 2.0 %copy.10 = bf16[128,2560]{1,0:T(8,128)(2,1)} copy(bf16[128,2560]{1,0:T(8,128)(2,1)} %shard_map.64) | data formatting | bytes 1310720

commit v3 on v1

v3 whole, which is shorter than its diff:
```python
import jax
import jax.numpy as jnp
from jax import lax
from jax.experimental import pallas as pl
from jax.experimental.pallas import tpu as pltpu
from jax.sharding import PartitionSpec as P

MESH = pl.DeviceIdType.MESH
CAP = 12
ORDER = (0, 1, 3, 2)


def layer(
    tokens,
    routes,
    scores,
    gate_hbm,
    up_hbm,
    down_hbm,
    out,
    gate,
    up,
    down,
    codes,
    other_codes,
    partner_tokens,
    below,
    above,
    place,
    outgoing,
    outgoing_side,
    rows_in,
    lhs,
    hidden,
    partials,
    arrived,
    returned,
    returned_side,
    cross_out,
    cross_in,
    side_out,
    side_in,
    sides,
    home,
    weight_sem,
    pair_s,
    pair_r,
    code_s,
    code_r,
    give_s,
    give_r,
    zx_s,
    zx_r,
    fwd_s,
    fwd_r,
    sum_s,
    sum_r,
    back_s,
    back_r,
    home_s,
    home_r,
):
    e, y = lax.axis_index("expert"), lax.axis_index("etp")
    core, x, z = e % 2, (e // 2) % 4, e // 8
    tok, features = tokens.shape
    half = features // 2
    a, b = pl.ds(0, half), pl.ds(half, half)
    slots = place.shape[1]
    group = slots // 4
    pe = e + 1 - 2 * core
    y_up, y_down = (y + 1) % 4, (y + 3) % 4
    partner, ups, downs = (pe, y), (e, y_up), (e, y_down)

    def owner(dz, dx):
        return ((((z + dz) % 4) * 4 + (x + dx) % 4) * 2 + core, y)

    def remote(src, dst, send, recv, to):
        return pltpu.make_async_remote_copy(
            src_ref=src, dst_ref=dst, send_sem=send, recv_sem=recv, device_id=to, device_id_type=MESH
        )

    weights = [
        pltpu.make_async_copy(gate_hbm, gate, weight_sem.at[0]),
        pltpu.make_async_copy(up_hbm, up, weight_sem.at[1]),
        pltpu.make_async_copy(down_hbm, down, weight_sem.at[2]),
    ]
    code_peers = (partner, ups, (pe, y_up), downs, (pe, y_down))
    barrier = pltpu.get_barrier_semaphore()
    peers = list(code_peers) + [owner(dz, dx) for dz in range(4) for dx in range(4) if dz or dx]
    for peer in peers:
        pl.semaphore_signal(barrier, inc=1, device_id=peer, device_id_type=MESH)
    for w in weights:
        w.start()

    first = lax.broadcasted_iota(jnp.int32, (tok, tok), 0)
    second = lax.broadcasted_iota(jnp.int32, (tok, tok), 1)
    route = routes[...]
    route_rows = jnp.broadcast_to(route.astype(jnp.float32), (tok, tok))
    same = route_rows == route_rows.T
    position = jnp.sum(jnp.where(same & (first < second), 1.0, 0.0), axis=0, keepdims=True)
    chip = ((route // 8 - z) & 3) * 4 + ((route // 2 - x) & 3)
    base = (route & 1) * 1024 + chip * (2 * CAP) + core * CAP
    codes[...] = jnp.broadcast_to(base.astype(jnp.float32) + position, codes.shape)

    pl.semaphore_wait(barrier, len(peers))
    swap_tokens = remote(tokens, partner_tokens, pair_s.at[0], pair_r.at[0], partner)
    swap_tokens.start()
    give_up = remote(tokens.at[:, a], below.at[0], give_s.at[0], give_r.at[0], ups)
    give_down = remote(tokens.at[:, b], above.at[0], give_s.at[1], give_r.at[1], downs)
    give_codes = [
        remote(codes, other_codes.at[i], code_s.at[i], code_r.at[i], peer)
        for i, peer in enumerate(code_peers)
    ]
    for g in give_codes:
        g.start()
    give_up.start()
    give_down.start()

    slot = lax.broadcasted_iota(jnp.int32, (slots, tok), 0)
    shift = core * 1024

    def marks(code):
        return jnp.where(slot == code.astype(jnp.int32) - shift, 1.0, 0.0).astype(jnp.bfloat16)

    place[0, :, 0:tok] = marks(codes[0:1, :])
    for i, (k, c) in enumerate(((0, 1), (1, 0), (1, 1), (2, 0), (2, 1))):
        give_codes[i].wait_recv()
        place[k, :, c * tok : (c + 1) * tok] = marks(other_codes[i, 0:1, :])
    swap_tokens.wait_recv()

    def zx_refs(kind, dz, dx, n):
        o, s = (4 - dz) % 4, (4 - dx) % 4
        src, dst = pl.ds(3 * dx, n), pl.ds(3 * s, n)
        if kind == 0:
            return outgoing.at[dz, src], rows_in.at[o, 0, dst]
        if kind == 1:
            return outgoing_side.at[0, dz, src], rows_in.at[o, 3, dst, :, a]
        return outgoing_side.at[1, dz, src], rows_in.at[o, 1, dst, :, b]

    def send_zx(kind, dz, dx):
        src, dst = zx_refs(kind, dz, dx, 3)
        k = ((4 - dz) % 4) * 3 + kind
        return remote(src, dst, zx_s.at[k], zx_r.at[k], owner(dz, dx))

    def all_zx(kind, o):
        if o:
            refs = zx_refs(kind, (4 - o) % 4, 0, 12)
        else:
            src = outgoing.at[0, pl.ds(3, 9)] if kind == 0 else outgoing_side.at[kind - 1, 0, pl.ds(3, 9)]
            part = pl.ds(3, 9)
            dst = (
                rows_in.at[0, 0, part]
                if kind == 0
                else rows_in.at[0, 3, part, :, a]
                if kind == 1
                else rows_in.at[0, 1, part, :, b]
            )
            refs = src, dst
        k = o * 3 + kind
        return remote(*refs, zx_s.at[k], zx_r.at[k], owner(0, 1))

    def forward(o, k):
        src, dst, to = (
            (rows_in.at[o, 0, :, :, a], rows_in.at[o, 1, :, :, a], downs),
            (rows_in.at[o, 0, :, :, b], rows_in.at[o, 3, :, :, b], ups),
            (rows_in.at[o, 3, :, :, a], rows_in.at[o, 2, :, :, a], ups),
            (rows_in.at[o, 1, :, :, b], rows_in.at[o, 2, :, :, b], downs),
        )[k]
        return remote(src, dst, fwd_s.at[o * 4 + k], fwd_r.at[o * 4 + k], to)

    def send_sum(o, k):
        src, to = (
            (partials.at[o, 1, :, :, a], ups),
            (partials.at[o, 3, :, :, b], downs),
            (partials.at[o, 2, :, :, a], downs),
            (partials.at[o, 2, :, :, b], ups),
        )[k]
        return remote(src, arrived.at[o, k], sum_s.at[o * 4 + k], sum_r.at[o * 4 + k], to)

    def back_refs(kind, o, dx, n):
        v, s = (4 - o) % 4, (4 - dx) % 4
        src, dst = pl.ds(3 * dx, n), pl.ds(3 * s, n)
        if kind == 0:
            return partials.at[o, 0, src], returned.at[v, dst]
        if kind == 1:
            return partials.at[o, 3, src, :, a], returned_side.at[0, v, dst]
        return partials.at[o, 1, src, :, b], returned_side.at[1, v, dst]

    def send_back(kind, o, dx):
        src, dst = back_refs(kind, o, dx, 3)
        k = ((4 - o) % 4) * 3 + kind
        return remote(src, dst, back_s.at[k], back_r.at[k], owner(o, dx))

    def all_back(kind, v):
        if v:
            refs = back_refs(kind, (4 - v) % 4, 0, 12)
        else:
            part = pl.ds(3, 9)
            refs = (
                (partials.at[0, 0, part], returned.at[0, part])
                if kind == 0
                else (partials.at[0, 3, part, :, a], returned_side.at[0, 0, part])
                if kind == 1
                else (partials.at[0, 1, part, :, b], returned_side.at[1, 0, part])
            )
        k = v * 3 + kind
        return remote(*refs, back_s.at[k], back_r.at[k], owner(0, 1))

    def pick(k, dz, mine, theirs):
        mark = place[k, dz * group : (dz + 1) * group, :]
        got = jnp.dot(mark[:, 0:tok], mine, preferred_element_type=jnp.float32)
        got += jnp.dot(mark[:, tok:], theirs, preferred_element_type=jnp.float32)
        return got.astype(jnp.bfloat16).reshape(group // 8, 8, 256)

    def place_own(o):
        dz = (4 - o) % 4

        @pl.loop(0, features // 256)
        def _(n):
            cols = pl.ds(pl.multiple_of(n * 256, 256), 256)
            outgoing[dz, :, :, cols] = pick(0, dz, tokens[:, cols], partner_tokens[:, cols])

        for dx in (1, 3, 2, 0):
            if dz or dx:
                send_zx(0, dz, dx).start()
            else:
                rows_in[0, 0, 0:3] = outgoing[0, 0:3]

    def place_side(o):
        dz = (4 - o) % 4

        @pl.loop(0, half // 256)
        def _(n):
            cols = pl.ds(pl.multiple_of(n * 256, 256), 256)
            outgoing_side[0, dz, :, :, cols] = pick(1, dz, below[0, :, cols], below[1, :, cols])
            outgoing_side[1, dz, :, :, cols] = pick(2, dz, above[0, :, cols], above[1, :, cols])

        for dx in (1, 3, 2, 0):
            if dz or dx:
                send_zx(1, dz, dx).start()
                send_zx(2, dz, dx).start()
            else:
                rows_in[0, 3, 0:3, :, 0:half] = outgoing_side[0, 0, 0:3]
                rows_in[0, 1, 0:3, :, half:] = outgoing_side[1, 0, 0:3]

    def forward_own(o):
        all_zx(0, o).wait_recv()
        forward(o, 0).start()
        forward(o, 1).start()

    def forward_side(o):
        all_zx(1, o).wait_recv()
        forward(o, 2).start()
        all_zx(2, o).wait_recv()
        forward(o, 3).start()

    def compute(o):
        for k in range(4):
            forward(o, k).wait_recv()
        for k in range(4):
            lhs[k * group : (k + 1) * group, :] = rows_in[o, k].reshape(group, features)

        @pl.loop(0, hidden.shape[1] // 256)
        def _(n):
            cols = pl.ds(pl.multiple_of(n * 256, 256), 256)
            g = jnp.dot(lhs[...], gate[:, cols], preferred_element_type=jnp.float32)
            u = jnp.dot(lhs[...], up[:, cols], preferred_element_type=jnp.float32)
            hidden[:, cols] = (g / (1.0 + jnp.exp(-g)) * u).astype(jnp.bfloat16)

        @pl.loop(0, features // 256)
        def _(n):
            cols = pl.ds(pl.multiple_of(n * 256, 256), 256)
            p = jnp.dot(hidden[...], down[:, cols], preferred_element_type=jnp.float32)
            partials[o, :, :, :, cols] = p.astype(jnp.bfloat16).reshape(4, group // 8, 8, 256)

        for k in range(4):
            send_sum(o, k).start()

    def finish(o):
        f32 = jnp.float32

        def added(k, part, cols, which):
            return (partials[o, k, part, :, cols].astype(f32) + arrived[o, which, part].astype(f32)).astype(
                jnp.bfloat16
            )

        for which in range(4):
            send_sum(o, which).wait_recv()
        for dx in (1, 3, 2, 0):
            part = pl.ds(3 * dx, 3)
            partials[o, 0, part, :, a] = added(0, part, a, 0)
            partials[o, 0, part, :, b] = added(0, part, b, 1)
            partials[o, 3, part, :, a] = added(3, part, a, 2)
            partials[o, 1, part, :, b] = added(1, part, b, 3)
            if o or dx:
                for kind in (1, 2, 0):
                    send_back(kind, o, dx).start()
            else:
                returned[0, 0:3] = partials[0, 0, 0:3]
                returned_side[0, 0, 0:3] = partials[0, 3, 0:3, :, 0:half]
                returned_side[1, 0, 0:3] = partials[0, 1, 0:3, :, half:]

    place_own(ORDER[0])
    give_up.wait_recv()
    swap_below = remote(below.at[0], below.at[1], pair_s.at[2], pair_r.at[2], partner)
    swap_below.start()
    give_down.wait_recv()
    swap_above = remote(above.at[0], above.at[1], pair_s.at[3], pair_r.at[3], partner)
    swap_above.start()
    place_own(ORDER[1])
    swap_below.wait_recv()
    swap_above.wait_recv()
    place_side(ORDER[0])
    forward_own(ORDER[0])
    place_own(ORDER[2])
    place_side(ORDER[1])
    forward_own(ORDER[1])
    forward_side(ORDER[0])
    place_own(ORDER[3])
    place_side(ORDER[2])
    place_side(ORDER[3])
    for w in weights:
        w.wait()
    for i, o in enumerate(ORDER):
        compute(o)
        if i + 1 < 4:
            forward_side(ORDER[i + 1])
        if i + 2 < 4:
            forward_own(ORDER[i + 2])
        if i >= 1:
            finish(ORDER[i - 1])
    finish(ORDER[3])

    slot_lane = lax.broadcasted_iota(jnp.int32, (tok, slots), 1)

    def picks(code_row):
        code = jnp.broadcast_to(code_row, (tok, tok)).T[:, 0:1].astype(jnp.int32)
        return jnp.where(slot_lane == code - shift, 1.0, 0.0).astype(jnp.bfloat16)

    def picked(code_row, source):
        return jnp.dot(picks(code_row), source, preferred_element_type=jnp.float32)

    for v in range(4):
        all_back(1, v).wait_recv()
        all_back(2, v).wait_recv()
    for v in range(4):
        rows = slice(v * group, (v + 1) * group)
        lhs[rows, 0:half] = returned_side[0, v].reshape(group, half)
        lhs[rows, half:] = returned_side[1, v].reshape(group, half)
    side_out[0] = picked(other_codes[2, 0:1, :], lhs[:, 0:half]).astype(jnp.bfloat16)
    swap_side_a = remote(side_out.at[0], side_in.at[0], pair_s.at[4], pair_r.at[4], partner)
    swap_side_a.start()
    side_out[1] = picked(other_codes[4, 0:1, :], lhs[:, half:]).astype(jnp.bfloat16)
    swap_side_b = remote(side_out.at[1], side_in.at[1], pair_s.at[5], pair_r.at[5], partner)
    swap_side_b.start()
    mine_a = picked(other_codes[1, 0:1, :], lhs[:, 0:half])
    swap_side_a.wait_recv()
    sides[0] = (mine_a + side_in[0].astype(jnp.float32)).astype(jnp.bfloat16)
    home_down = remote(sides.at[0], home.at[0], home_s.at[0], home_r.at[0], downs)
    home_down.start()
    mine_b = picked(other_codes[3, 0:1, :], lhs[:, half:])
    swap_side_b.wait_recv()
    sides[1] = (mine_b + side_in[1].astype(jnp.float32)).astype(jnp.bfloat16)
    home_up = remote(sides.at[1], home.at[1], home_s.at[1], home_r.at[1], ups)
    home_up.start()
    for v in range(4):
        all_back(0, v).wait_recv()
    for v in range(4):
        lhs[v * group : (v + 1) * group, :] = returned[v].reshape(group, features)
    cross_out[...] = picked(other_codes[0, 0:1, :], lhs[...]).astype(jnp.bfloat16)
    swap_back = remote(cross_out, cross_in, pair_s.at[1], pair_r.at[1], partner)
    swap_back.start()
    mine = picked(codes[0:1, :], lhs[...])
    score = jnp.broadcast_to(scores[...], (tok, tok)).T[:, 0:1]
    swap_back.wait_recv()
    home_down.wait_recv()
    out[:, 0:half] = (
        score * (mine[:, 0:half] + cross_in[:, 0:half].astype(jnp.float32) + home[0].astype(jnp.float32))
    ).astype(jnp.bfloat16)
    home_up.wait_recv()
    out[:, half:] = (
        score * (mine[:, half:] + cross_in[:, half:].astype(jnp.float32) + home[1].astype(jnp.float32))
    ).astype(jnp.bfloat16)

    for c in (
        swap_tokens,
        give_up,
        give_down,
        swap_below,
        swap_above,
        swap_side_a,
        swap_side_b,
        home_down,
        home_up,
        swap_back,
        *give_codes,
    ):
        c.wait_send()
    for o in range(4):
        for kind in range(3):
            all_zx(kind, o).wait_send()
            all_back(kind, o).wait_send()
        for k in range(4):
            forward(o, k).wait_send()
            send_sum(o, k).wait_send()


def local(tokens, routes, scores, gate_weight, up_weight, down_weight):
    tok, features = tokens.shape
    hid = gate_weight.shape[2]
    half = features // 2
    slots = 32 * CAP
    group = slots // 4
    g8 = group // 8
    bf = jnp.bfloat16
    vmem = pl.BlockSpec(memory_space=pltpu.VMEM)
    hbm = pl.BlockSpec(memory_space=pl.ANY)
    sizes = (
        (features, hid),
        (features, hid),
        (hid, features),
        None,
        None,
        (tok, features),
        (2, tok, half),
        (2, tok, half),
        (3, slots, 2 * tok),
        (4, g8, 8, features),
        (2, 4, g8, 8, half),
        (4, 4, g8, 8, features),
        (slots, features),
        (slots, hid),
        (4, 4, g8, 8, features),
        (4, 4, g8, 8, half),
        (4, g8, 8, features),
        (2, 4, g8, 8, half),
        (tok, features),
        (tok, features),
        (2, tok, half),
        (2, tok, half),
        (2, tok, half),
        (2, tok, half),
    )
    scratch = [pltpu.VMEM(s, bf) if s else None for s in sizes]
    scratch[3] = pltpu.VMEM((8, tok), jnp.float32)
    scratch[4] = pltpu.VMEM((5, 8, tok), jnp.float32)
    counts = (3, 6, 6, 5, 5, 2, 2, 12, 12, 16, 16, 16, 16, 12, 12, 2, 2)
    return pl.pallas_call(
        layer,
        out_shape=jax.ShapeDtypeStruct((tok, features), bf),
        in_specs=[vmem] * 3 + [hbm] * 3,
        out_specs=vmem,
        scratch_shapes=scratch + [pltpu.SemaphoreType.DMA((n,)) for n in counts],
        compiler_params=pltpu.CompilerParams(
            collective_id=0, has_side_effects=True, vmem_limit_bytes=62 * 1024 * 1024
        ),
    )(
        tokens,
        routes.reshape(1, tok),
        scores.reshape(1, tok),
        gate_weight[0],
        up_weight[0],
        down_weight[0],
    )


def solution(mesh):
    in_specs = (
        P(("expert", "etp"), None),
        P(("expert", "etp"), None),
        P(("expert", "etp")),
        P("expert", None, "etp"),
        P("expert", None, "etp"),
        P("expert", "etp", None),
    )
    out_specs = P(("expert", "etp"), None)
    return jax.shard_map(local, mesh=mesh, in_specs=in_specs, out_specs=out_specs, check_vma=False)
```

time: 309 us -> 178 us (0.58)
  Pallas kernels: 0 us -> 176 us
  waiting for transfers between devices: 155 us -> 0 us
  blocking collectives: 81.5 us -> 0 us
  matrix products: 42.5 us -> 0 us
  between operations: 13.4 us -> 0.01 us
  local copies, waits for them, and re-layouts: 11.7 us -> 1.97 us
    pallas_call x0 -> x1, Pallas kernels: none -> 176 us  [local(): pl.pallas_call(layer, out_shape=jax.ShapeDtypeStruct((tok, features), bf)...]
    all_to_all x2 -> x0, blocking collectives: 81.5 us -> none  [the longest x1 41.1 us: local(): lax.all_to_all(outgoing, 'expert', split_axis=0, concat_axis=0, tiled=True)]
    reduce_scatter x1 -> x0, waiting for transfers between devices: 77.9 us -> none  [local(): lax.psum_scatter(partial_value, 'etp', scatter_dimension=0, tiled=True)]
    all_gather x1 -> x0, waiting for transfers between devices: 77.5 us -> none  [local(): lax.all_gather(received.reshape(experts * slot_count, features), 'etp', a...]
    dot_general x4 -> x0, matrix products: 42.5 us -> none  [the longest x1 25.3 us: local(): jnp.dot(hidden, down_local, preferred_element_type=jnp.float32)]
    reshape x4 -> x0, local copies, waits for them, and re-layouts: 11.6 us -> none  [the longest x1 4.04 us: local(): received.reshape(experts * slot_count, features)]
  transfers between devices with their start and end apart: 2 -> 0, of which waited for: 2 -> 0; matrix products, arithmetic and copies ran while one was open for 0% -> 0% of each run, Pallas kernels for 0% -> 0%
where the time goes in v3:
time: 178 us
  Pallas kernels  176 us (99%)
  local copies, waits for them, and re-layouts  1.97 us (1%)
    pallas_call x1, Pallas kernels, local(): pl.pallas_call(layer, out_shape=jax.ShapeDtypeStruct((tok, features), bf)...  176 us

profile of v3, /device:TPU:33, one launch (start us, length us, event | category | flops | bytes accessed | tf_op | source)
XLA Modules:
  0.0 177.7 jit_solution(203347477208076701)
XLA Ops:
  0.0 175.7 %shard_map.64 = bf16[128,2560]{1,0:T(8,128)(2,1)} custom-call(bf16[128,2560]{1,0:T(8,128)(2,1)} %tokens.1, s32[1,128]{1,0:T(1,128)} %bitcast.8, f32[1,128]{1,0:T(1,128)} %bitcast.9, bf16[2560,1024]{1,0:T(8,128)(2,1)} %bitcast.5, bf16[2560,1024]{1,0:T(8,128)(2,1)} %bitcast.6, bf16[1024,2560]{1,0:T(8,128)(2,1)} %bitcast.7), custom_call_target="tpu_custom_call" | custom-call | tf_op jit(solution)/shard_map/pallas_call | solution.py:448
  175.7 2.0 %copy.8 = bf16[128,2560]{1,0:T(8,128)(2,1)} copy(bf16[128,2560]{1,0:T(8,128)(2,1)} %shard_map.64) | data formatting | bytes 1310720

commit v4 on v3

--- a/solution.py
+++ b/solution.py
@@ -42,6 +42,7 @@
     side_in,
     sides,
     home,
+    passed,
     weight_sem,
     pair_s,
     pair_r,
@@ -59,6 +60,8 @@
     back_r,
     home_s,
     home_r,
+    pass_s,
+    pass_r,
 ):
     e, y = lax.axis_index("expert"), lax.axis_index("etp")
     core, x, z = e % 2, (e // 2) % 4, e // 8
@@ -86,7 +89,7 @@
     ]
     code_peers = (partner, ups, (pe, y_up), downs, (pe, y_down))
     barrier = pltpu.get_barrier_semaphore()
-    peers = list(code_peers) + [owner(dz, dx) for dz in range(4) for dx in range(4) if dz or dx]
+    peers = [owner(dz, dx) for dz in range(4) for dx in range(4) if dz or dx] + list(code_peers)
     for peer in peers:
         pl.semaphore_signal(barrier, inc=1, device_id=peer, device_id_type=MESH)
     for w in weights:
@@ -254,7 +257,7 @@
         all_zx(2, o).wait_recv()
         forward(o, 3).start()
 
-    def compute(o):
+    def compute(o, middle):
         for k in range(4):
             forward(o, k).wait_recv()
         for k in range(4):
@@ -267,6 +270,9 @@
             u = jnp.dot(lhs[...], up[:, cols], preferred_element_type=jnp.float32)
             hidden[:, cols] = (g / (1.0 + jnp.exp(-g)) * u).astype(jnp.bfloat16)
 
+        if middle is not None:
+            forward_side(middle)
+
         @pl.loop(0, features // 256)
         def _(n):
             cols = pl.ds(pl.multiple_of(n * 256, 256), 256)
@@ -276,22 +282,21 @@
         for k in range(4):
             send_sum(o, k).start()
 
+    def added(o, k, part, cols, addends):
+        total = partials[o, k, part, :, cols].astype(jnp.float32)
+        for addend in addends:
+            total += addend[part].astype(jnp.float32)
+        return total.astype(jnp.bfloat16)
+
     def finish(o):
-        f32 = jnp.float32
-
-        def added(k, part, cols, which):
-            return (partials[o, k, part, :, cols].astype(f32) + arrived[o, which, part].astype(f32)).astype(
-                jnp.bfloat16
-            )
-
         for which in range(4):
             send_sum(o, which).wait_recv()
         for dx in (1, 3, 2, 0):
             part = pl.ds(3 * dx, 3)
-            partials[o, 0, part, :, a] = added(0, part, a, 0)
-            partials[o, 0, part, :, b] = added(0, part, b, 1)
-            partials[o, 3, part, :, a] = added(3, part, a, 2)
-            partials[o, 1, part, :, b] = added(1, part, b, 3)
+            partials[o, 3, part, :, a] = added(o, 3, part, a, [arrived.at[o, 2]])
+            partials[o, 1, part, :, b] = added(o, 1, part, b, [arrived.at[o, 3]])
+            partials[o, 0, part, :, a] = added(o, 0, part, a, [arrived.at[o, 0]])
+            partials[o, 0, part, :, b] = added(o, 0, part, b, [arrived.at[o, 1]])
             if o or dx:
                 for kind in (1, 2, 0):
                     send_back(kind, o, dx).start()
@@ -300,36 +305,58 @@
                 returned_side[0, 0, 0:3] = partials[0, 3, 0:3, :, 0:half]
                 returned_side[1, 0, 0:3] = partials[0, 1, 0:3, :, half:]
 
+    last = ORDER[3]
+    pass_down = remote(partials.at[last, 3, :, :, a], passed.at[0], pass_s.at[0], pass_r.at[0], downs)
+    pass_up = remote(partials.at[last, 1, :, :, b], passed.at[1], pass_s.at[1], pass_r.at[1], ups)
+
+    def pass_sums():
+        everything = pl.ds(0, group // 8)
+        send_sum(last, 2).wait_recv()
+        partials[last, 3, :, :, a] = added(last, 3, everything, a, [arrived.at[last, 2]])
+        pass_down.start()
+        send_sum(last, 3).wait_recv()
+        partials[last, 1, :, :, b] = added(last, 1, everything, b, [arrived.at[last, 3]])
+        pass_up.start()
+
+    def finish_last():
+        send_sum(last, 0).wait_recv()
+        send_sum(last, 1).wait_recv()
+        pass_down.wait_recv()
+        pass_up.wait_recv()
+        for dx in (1, 3, 2, 0):
+            part = pl.ds(3 * dx, 3)
+            partials[last, 0, part, :, a] = added(last, 0, part, a, [arrived.at[last, 0], passed.at[0]])
+            partials[last, 0, part, :, b] = added(last, 0, part, b, [arrived.at[last, 1], passed.at[1]])
+            send_back(0, last, dx).start()
+
     place_own(ORDER[0])
+    place_own(ORDER[1])
+    forward_own(ORDER[0])
     give_up.wait_recv()
     swap_below = remote(below.at[0], below.at[1], pair_s.at[2], pair_r.at[2], partner)
     swap_below.start()
     give_down.wait_recv()
     swap_above = remote(above.at[0], above.at[1], pair_s.at[3], pair_r.at[3], partner)
     swap_above.start()
-    place_own(ORDER[1])
+    place_own(ORDER[2])
     swap_below.wait_recv()
     swap_above.wait_recv()
     place_side(ORDER[0])
-    forward_own(ORDER[0])
-    place_own(ORDER[2])
     place_side(ORDER[1])
     forward_own(ORDER[1])
+    place_own(ORDER[3])
     forward_side(ORDER[0])
-    place_own(ORDER[3])
     place_side(ORDER[2])
     place_side(ORDER[3])
     for w in weights:
         w.wait()
     for i, o in enumerate(ORDER):
-        compute(o)
-        if i + 1 < 4:
-            forward_side(ORDER[i + 1])
         if i + 2 < 4:
             forward_own(ORDER[i + 2])
+        compute(o, ORDER[i + 1] if i + 1 < 4 else None)
         if i >= 1:
             finish(ORDER[i - 1])
-    finish(ORDER[3])
+    pass_sums()
 
     slot_lane = lax.broadcasted_iota(jnp.int32, (tok, slots), 1)
 
@@ -340,9 +367,11 @@
     def picked(code_row, source):
         return jnp.dot(picks(code_row), source, preferred_element_type=jnp.float32)
 
-    for v in range(4):
-        all_back(1, v).wait_recv()
-        all_back(2, v).wait_recv()
+    for o in ORDER[:3]:
+        all_back(1, (4 - o) % 4).wait_recv()
+        all_back(2, (4 - o) % 4).wait_recv()
+    unused = (4 - last) % 4
+    returned_side[:, unused] = jnp.zeros((2, group // 8, 8, half), jnp.bfloat16)
     for v in range(4):
         rows = slice(v * group, (v + 1) * group)
         lhs[rows, 0:half] = returned_side[0, v].reshape(group, half)
@@ -363,6 +392,7 @@
     sides[1] = (mine_b + side_in[1].astype(jnp.float32)).astype(jnp.bfloat16)
     home_up = remote(sides.at[1], home.at[1], home_s.at[1], home_r.at[1], ups)
     home_up.start()
+    finish_last()
     for v in range(4):
         all_back(0, v).wait_recv()
     for v in range(4):
@@ -393,13 +423,16 @@
         home_down,
         home_up,
         swap_back,
+        pass_down,
+        pass_up,
         *give_codes,
     ):
         c.wait_send()
     for o in range(4):
         for kind in range(3):
             all_zx(kind, o).wait_send()
-            all_back(kind, o).wait_send()
+            if kind == 0 or o != unused:
+                all_back(kind, o).wait_send()
         for k in range(4):
             forward(o, k).wait_send()
             send_sum(o, k).wait_send()
@@ -440,11 +473,12 @@
         (2, tok, half),
         (2, tok, half),
         (2, tok, half),
+        (2, g8, 8, half),
     )
     scratch = [pltpu.VMEM(s, bf) if s else None for s in sizes]
     scratch[3] = pltpu.VMEM((8, tok), jnp.float32)
     scratch[4] = pltpu.VMEM((5, 8, tok), jnp.float32)
-    counts = (3, 6, 6, 5, 5, 2, 2, 12, 12, 16, 16, 16, 16, 12, 12, 2, 2)
+    counts = (3, 6, 6, 5, 5, 2, 2, 12, 12, 16, 16, 16, 16, 12, 12, 2, 2, 2, 2)
     return pl.pallas_call(
         layer,
         out_shape=jax.ShapeDtypeStruct((tok, features), bf),

time: 178 us -> 148 us (0.83)
  Pallas kernels: 176 us -> 146 us
    pallas_call x1, Pallas kernels: 176 us -> 146 us  [local(): pl.pallas_call(layer, out_shape=jax.ShapeDtypeStruct((tok, features), bf)...]
where the time goes in v4:
time: 148 us
  Pallas kernels  146 us (99%)
  local copies, waits for them, and re-layouts  1.97 us (1%)
    pallas_call x1, Pallas kernels, local(): pl.pallas_call(layer, out_shape=jax.ShapeDtypeStruct((tok, features), bf)...  146 us

profile of v4, /device:TPU:33, one launch (start us, length us, event | category | flops | bytes accessed | tf_op | source)
XLA Modules:
  0.0 147.7 jit_solution(6473457929817992567)
XLA Ops:
  0.0 145.7 %shard_map.64 = bf16[128,2560]{1,0:T(8,128)(2,1)} custom-call(bf16[128,2560]{1,0:T(8,128)(2,1)} %tokens.1, s32[1,128]{1,0:T(1,128)} %bitcast.8, f32[1,128]{1,0:T(1,128)} %bitcast.9, bf16[2560,1024]{1,0:T(8,128)(2,1)} %bitcast.5, bf16[2560,1024]{1,0:T(8,128)(2,1)} %bitcast.6, bf16[1024,2560]{1,0:T(8,128)(2,1)} %bitcast.7), custom_call_target="tpu_custom_call" | custom-call | tf_op jit(solution)/shard_map/pallas_call | solution.py:482
  145.7 2.0 %copy.8 = bf16[128,2560]{1,0:T(8,128)(2,1)} copy(bf16[128,2560]{1,0:T(8,128)(2,1)} %shard_map.64) | data formatting | bytes 1310720

commit v5 on v4

--- a/solution.py
+++ b/solution.py
@@ -75,7 +75,7 @@
     partner, ups, downs = (pe, y), (e, y_up), (e, y_down)
 
     def owner(dz, dx):
-        return ((((z + dz) % 4) * 4 + (x + dx) % 4) * 2 + core, y)
+        return ((((z + dz + dx) % 4) * 4 + (x + dx) % 4) * 2 + core, y)
 
     def remote(src, dst, send, recv, to):
         return pltpu.make_async_remote_copy(
@@ -101,7 +101,8 @@
     route_rows = jnp.broadcast_to(route.astype(jnp.float32), (tok, tok))
     same = route_rows == route_rows.T
     position = jnp.sum(jnp.where(same & (first < second), 1.0, 0.0), axis=0, keepdims=True)
-    chip = ((route // 8 - z) & 3) * 4 + ((route // 2 - x) & 3)
+    chip_x = (route // 2 - x) & 3
+    chip = ((route // 8 - z - chip_x) & 3) * 4 + chip_x
     base = (route & 1) * 1024 + chip * (2 * CAP) + core * CAP
     codes[...] = jnp.broadcast_to(base.astype(jnp.float32) + position, codes.shape)
 
@@ -223,7 +224,7 @@
             cols = pl.ds(pl.multiple_of(n * 256, 256), 256)
             outgoing[dz, :, :, cols] = pick(0, dz, tokens[:, cols], partner_tokens[:, cols])
 
-        for dx in (1, 3, 2, 0):
+        for dx in (2, 1, 3, 0):
             if dz or dx:
                 send_zx(0, dz, dx).start()
             else:
@@ -238,7 +239,7 @@
             outgoing_side[0, dz, :, :, cols] = pick(1, dz, below[0, :, cols], below[1, :, cols])
             outgoing_side[1, dz, :, :, cols] = pick(2, dz, above[0, :, cols], above[1, :, cols])
 
-        for dx in (1, 3, 2, 0):
+        for dx in (2, 1, 3, 0):
             if dz or dx:
                 send_zx(1, dz, dx).start()
                 send_zx(2, dz, dx).start()
@@ -279,7 +280,7 @@
             p = jnp.dot(hidden[...], down[:, cols], preferred_element_type=jnp.float32)
             partials[o, :, :, :, cols] = p.astype(jnp.bfloat16).reshape(4, group // 8, 8, 256)
 
-        for k in range(4):
+        for k in (2, 3, 0, 1):
             send_sum(o, k).start()
 
     def added(o, k, part, cols, addends):
@@ -291,7 +292,7 @@
     def finish(o):
         for which in range(4):
             send_sum(o, which).wait_recv()
-        for dx in (1, 3, 2, 0):
+        for dx in (2, 1, 3, 0):
             part = pl.ds(3 * dx, 3)
             partials[o, 3, part, :, a] = added(o, 3, part, a, [arrived.at[o, 2]])
             partials[o, 1, part, :, b] = added(o, 1, part, b, [arrived.at[o, 3]])
@@ -306,6 +307,7 @@
                 returned_side[1, 0, 0:3] = partials[0, 1, 0:3, :, half:]
 
     last = ORDER[3]
+    unused = (4 - last) % 4
     pass_down = remote(partials.at[last, 3, :, :, a], passed.at[0], pass_s.at[0], pass_r.at[0], downs)
     pass_up = remote(partials.at[last, 1, :, :, b], passed.at[1], pass_s.at[1], pass_r.at[1], ups)
 
@@ -323,7 +325,7 @@
         send_sum(last, 1).wait_recv()
         pass_down.wait_recv()
         pass_up.wait_recv()
-        for dx in (1, 3, 2, 0):
+        for dx in (2, 1, 3, 0):
             part = pl.ds(3 * dx, 3)
             partials[last, 0, part, :, a] = added(last, 0, part, a, [arrived.at[last, 0], passed.at[0]])
             partials[last, 0, part, :, b] = added(last, 0, part, b, [arrived.at[last, 1], passed.at[1]])
@@ -367,10 +369,14 @@
     def picked(code_row, source):
         return jnp.dot(picks(code_row), source, preferred_element_type=jnp.float32)
 
+    def picked_last(code_row, source):
+        return jnp.dot(
+            picks(code_row)[:, unused * group : (unused + 1) * group], source, preferred_element_type=jnp.float32
+        )
+
     for o in ORDER[:3]:
         all_back(1, (4 - o) % 4).wait_recv()
         all_back(2, (4 - o) % 4).wait_recv()
-    unused = (4 - last) % 4
     returned_side[:, unused] = jnp.zeros((2, group // 8, 8, half), jnp.bfloat16)
     for v in range(4):
         rows = slice(v * group, (v + 1) * group)
@@ -392,15 +398,21 @@
     sides[1] = (mine_b + side_in[1].astype(jnp.float32)).astype(jnp.bfloat16)
     home_up = remote(sides.at[1], home.at[1], home_s.at[1], home_r.at[1], ups)
     home_up.start()
+    for o in ORDER[:3]:
+        all_back(0, (4 - o) % 4).wait_recv()
+    for v in range(4):
+        rows = slice(v * group, (v + 1) * group)
+        lhs[rows, :] = jnp.zeros((group, features), lhs.dtype) if v == unused else returned[v].reshape(group, features)
+    theirs = picked(other_codes[0, 0:1, :], lhs[...])
+    mine = picked(codes[0:1, :], lhs[...])
     finish_last()
-    for v in range(4):
-        all_back(0, v).wait_recv()
-    for v in range(4):
-        lhs[v * group : (v + 1) * group, :] = returned[v].reshape(group, features)
-    cross_out[...] = picked(other_codes[0, 0:1, :], lhs[...]).astype(jnp.bfloat16)
+    all_back(0, unused).wait_recv()
+    lhs[0:group, :] = returned[unused].reshape(group, features)
+    theirs += picked_last(other_codes[0, 0:1, :], lhs[0:group, :])
+    cross_out[...] = theirs.astype(jnp.bfloat16)
     swap_back = remote(cross_out, cross_in, pair_s.at[1], pair_r.at[1], partner)
     swap_back.start()
-    mine = picked(codes[0:1, :], lhs[...])
+    mine += picked_last(codes[0:1, :], lhs[0:group, :])
     score = jnp.broadcast_to(scores[...], (tok, tok)).T[:, 0:1]
     swap_back.wait_recv()
     home_down.wait_recv()

time: 148 us -> 140 us (0.946); the launches traced: 148 us -> 137 us
  Pallas kernels: 146 us -> 135 us
    pallas_call x1, Pallas kernels: 146 us -> 135 us  [local(): pl.pallas_call(layer, out_shape=jax.ShapeDtypeStruct((tok, features), bf)...]
where the time goes in v5:
time: 140 us; the launch traced here: 137 us
  Pallas kernels  135 us (96%)
  local copies, waits for them, and re-layouts  1.97 us (1%)
    pallas_call x1, Pallas kernels, local(): pl.pallas_call(layer, out_shape=jax.ShapeDtypeStruct((tok, features), bf)...  135 us

profile of v5, /device:TPU:33, one launch (start us, length us, event | category | flops | bytes accessed | tf_op | source)
XLA Modules:
  0.0 136.9 jit_solution(10247306581499357412)
XLA Ops:
  0.0 135.0 %shard_map.64 = bf16[128,2560]{1,0:T(8,128)(2,1)} custom-call(bf16[128,2560]{1,0:T(8,128)(2,1)} %tokens.1, s32[1,128]{1,0:T(1,128)} %bitcast.8, f32[1,128]{1,0:T(1,128)} %bitcast.9, bf16[2560,1024]{1,0:T(8,128)(2,1)} %bitcast.5, bf16[2560,1024]{1,0:T(8,128)(2,1)} %bitcast.6, bf16[1024,2560]{1,0:T(8,128)(2,1)} %bitcast.7), custom_call_target="tpu_custom_call" | custom-call | tf_op jit(solution)/shard_map/pallas_call | solution.py:494
  135.0 2.0 %copy.8 = bf16[128,2560]{1,0:T(8,128)(2,1)} copy(bf16[128,2560]{1,0:T(8,128)(2,1)} %shard_map.64) | data formatting | bytes 1310720

commit v6 on v5

--- a/solution.py
+++ b/solution.py
@@ -127,9 +127,8 @@
         return jnp.where(slot == code.astype(jnp.int32) - shift, 1.0, 0.0).astype(jnp.bfloat16)
 
     place[0, :, 0:tok] = marks(codes[0:1, :])
-    for i, (k, c) in enumerate(((0, 1), (1, 0), (1, 1), (2, 0), (2, 1))):
-        give_codes[i].wait_recv()
-        place[k, :, c * tok : (c + 1) * tok] = marks(other_codes[i, 0:1, :])
+    give_codes[0].wait_recv()
+    place[0, :, tok : 2 * tok] = marks(other_codes[0, 0:1, :])
     swap_tokens.wait_recv()
 
     def zx_refs(kind, dz, dx, n):
@@ -214,14 +213,12 @@
         mark = place[k, dz * group : (dz + 1) * group, :]
         got = jnp.dot(mark[:, 0:tok], mine, preferred_element_type=jnp.float32)
         got += jnp.dot(mark[:, tok:], theirs, preferred_element_type=jnp.float32)
-        return got.astype(jnp.bfloat16).reshape(group // 8, 8, 256)
+        return got.astype(jnp.bfloat16).reshape(group // 8, 8, half)
 
     def place_own(o):
         dz = (4 - o) % 4
 
-        @pl.loop(0, features // 256)
-        def _(n):
-            cols = pl.ds(pl.multiple_of(n * 256, 256), 256)
+        for cols in (a, b):
             outgoing[dz, :, :, cols] = pick(0, dz, tokens[:, cols], partner_tokens[:, cols])
 
         for dx in (2, 1, 3, 0):
@@ -233,11 +230,8 @@
     def place_side(o):
         dz = (4 - o) % 4
 
-        @pl.loop(0, half // 256)
-        def _(n):
-            cols = pl.ds(pl.multiple_of(n * 256, 256), 256)
-            outgoing_side[0, dz, :, :, cols] = pick(1, dz, below[0, :, cols], below[1, :, cols])
-            outgoing_side[1, dz, :, :, cols] = pick(2, dz, above[0, :, cols], above[1, :, cols])
+        outgoing_side[0, dz] = pick(1, dz, below[0], below[1])
+        outgoing_side[1, dz] = pick(2, dz, above[0], above[1])
 
         for dx in (2, 1, 3, 0):
             if dz or dx:
@@ -272,6 +266,8 @@
             hidden[:, cols] = (g / (1.0 + jnp.exp(-g)) * u).astype(jnp.bfloat16)
 
         if middle is not None:
+            if middle == ORDER[2]:
+                forward_own(ORDER[3])
             forward_side(middle)
 
         @pl.loop(0, features // 256)
@@ -333,6 +329,9 @@
 
     place_own(ORDER[0])
     place_own(ORDER[1])
+    for i, (k, c) in enumerate(((1, 0), (1, 1), (2, 0), (2, 1))):
+        give_codes[i + 1].wait_recv()
+        place[k, :, c * tok : (c + 1) * tok] = marks(other_codes[i + 1, 0:1, :])
     forward_own(ORDER[0])
     give_up.wait_recv()
     swap_below = remote(below.at[0], below.at[1], pair_s.at[2], pair_r.at[2], partner)
@@ -353,9 +352,10 @@
     for w in weights:
         w.wait()
     for i, o in enumerate(ORDER):
-        if i + 2 < 4:
-            forward_own(ORDER[i + 2])
-        compute(o, ORDER[i + 1] if i + 1 < 4 else None)
+        if i == 0:
+            forward_own(ORDER[2])
+            forward_side(ORDER[1])
+        compute(o, ORDER[i + 2] if i + 2 < 4 else None)
         if i >= 1:
             finish(ORDER[i - 1])
     pass_sums()

time: 140 us -> 137 us (0.979)
  Pallas kernels: 135 us -> 133 us
    pallas_call x1, Pallas kernels: 135 us -> 133 us  [local(): pl.pallas_call(layer, out_shape=jax.ShapeDtypeStruct((tok, features), bf)...]
where the time goes in v6:
time: 137 us; the launch traced here: 135 us
  Pallas kernels  133 us (97%)
  local copies, waits for them, and re-layouts  1.97 us (1%)
    pallas_call x1, Pallas kernels, local(): pl.pallas_call(layer, out_shape=jax.ShapeDtypeStruct((tok, features), bf)...  133 us

profile of v6, /device:TPU:33, one launch (start us, length us, event | category | flops | bytes accessed | tf_op | source)
XLA Modules:
  0.0 135.1 jit_solution(17781629315624076766)
XLA Ops:
  0.0 133.1 %shard_map.64 = bf16[128,2560]{1,0:T(8,128)(2,1)} custom-call(bf16[128,2560]{1,0:T(8,128)(2,1)} %tokens.1, s32[1,128]{1,0:T(1,128)} %bitcast.8, f32[1,128]{1,0:T(1,128)} %bitcast.9, bf16[2560,1024]{1,0:T(8,128)(2,1)} %bitcast.5, bf16[2560,1024]{1,0:T(8,128)(2,1)} %bitcast.6, bf16[1024,2560]{1,0:T(8,128)(2,1)} %bitcast.7), custom_call_target="tpu_custom_call" | custom-call | tf_op jit(solution)/shard_map/pallas_call | solution.py:494
  133.1 2.0 %copy.8 = bf16[128,2560]{1,0:T(8,128)(2,1)} copy(bf16[128,2560]{1,0:T(8,128)(2,1)} %shard_map.64) | data formatting | bytes 1310720

commit v7 on v6

--- a/solution.py
+++ b/solution.py
@@ -270,14 +270,16 @@
                 forward_own(ORDER[3])
             forward_side(middle)
 
-        @pl.loop(0, features // 256)
-        def _(n):
-            cols = pl.ds(pl.multiple_of(n * 256, 256), 256)
-            p = jnp.dot(hidden[...], down[:, cols], preferred_element_type=jnp.float32)
-            partials[o, :, :, :, cols] = p.astype(jnp.bfloat16).reshape(4, group // 8, 8, 256)
-
-        for k in (2, 3, 0, 1):
-            send_sum(o, k).start()
+        for side in (0, 1):
+
+            @pl.loop(side * half // 256, (side + 1) * half // 256)
+            def _(n):
+                cols = pl.ds(pl.multiple_of(n * 256, 256), 256)
+                p = jnp.dot(hidden[...], down[:, cols], preferred_element_type=jnp.float32)
+                partials[o, :, :, :, cols] = p.astype(jnp.bfloat16).reshape(4, group // 8, 8, 256)
+
+            send_sum(o, 2 + side).start()
+            send_sum(o, side).start()
 
     def added(o, k, part, cols, addends):
         total = partials[o, k, part, :, cols].astype(jnp.float32)
@@ -356,8 +358,9 @@
             forward_own(ORDER[2])
             forward_side(ORDER[1])
         compute(o, ORDER[i + 2] if i + 2 < 4 else None)
-        if i >= 1:
-            finish(ORDER[i - 1])
+        if i >= 2:
+            finish(ORDER[i - 2])
+    finish(ORDER[2])
     pass_sums()
 
     slot_lane = lax.broadcasted_iota(jnp.int32, (tok, slots), 1)

time: 137 us -> 137 us (level)
  no operation moved by 1% of the time
where the time goes in v7:
time: 137 us; the launch traced here: 135 us
  Pallas kernels  133 us (97%)
  local copies, waits for them, and re-layouts  1.97 us (1%)
    pallas_call x1, Pallas kernels, local(): pl.pallas_call(layer, out_shape=jax.ShapeDtypeStruct((tok, features), bf)...  133 us

profile of v7, /device:TPU:33, one launch (start us, length us, event | category | flops | bytes accessed | tf_op | source)
XLA Modules:
  0.0 135.5 jit_solution(822921051611720965)
XLA Ops:
  0.0 133.5 %shard_map.64 = bf16[128,2560]{1,0:T(8,128)(2,1)} custom-call(bf16[128,2560]{1,0:T(8,128)(2,1)} %tokens.1, s32[1,128]{1,0:T(1,128)} %bitcast.8, f32[1,128]{1,0:T(1,128)} %bitcast.9, bf16[2560,1024]{1,0:T(8,128)(2,1)} %bitcast.5, bf16[2560,1024]{1,0:T(8,128)(2,1)} %bitcast.6, bf16[1024,2560]{1,0:T(8,128)(2,1)} %bitcast.7), custom_call_target="tpu_custom_call" | custom-call | tf_op jit(solution)/shard_map/pallas_call | solution.py:497
  133.5 2.0 %copy.8 = bf16[128,2560]{1,0:T(8,128)(2,1)} copy(bf16[128,2560]{1,0:T(8,128)(2,1)} %shard_map.64) | data formatting | bytes 1310720

commit v8 on v7

--- a/solution.py
+++ b/solution.py
@@ -115,10 +115,10 @@
         remote(codes, other_codes.at[i], code_s.at[i], code_r.at[i], peer)
         for i, peer in enumerate(code_peers)
     ]
+    give_up.start()
+    give_down.start()
     for g in give_codes:
         g.start()
-    give_up.start()
-    give_down.start()
 
     slot = lax.broadcasted_iota(jnp.int32, (slots, tok), 0)
     shift = core * 1024

time: 137 us -> 137 us (level)
  no operation moved by 1% of the time
where the time goes in v8:
time: 137 us; the launch traced here: 135 us
  Pallas kernels  133 us (97%)
  local copies, waits for them, and re-layouts  1.97 us (1%)
    pallas_call x1, Pallas kernels, local(): pl.pallas_call(layer, out_shape=jax.ShapeDtypeStruct((tok, features), bf)...  133 us

profile of v8, /device:TPU:33, one launch (start us, length us, event | category | flops | bytes accessed | tf_op | source)
XLA Modules:
  0.0 135.5 jit_solution(13273679986090477088)
XLA Ops:
  0.0 133.5 %shard_map.64 = bf16[128,2560]{1,0:T(8,128)(2,1)} custom-call(bf16[128,2560]{1,0:T(8,128)(2,1)} %tokens.1, s32[1,128]{1,0:T(1,128)} %bitcast.8, f32[1,128]{1,0:T(1,128)} %bitcast.9, bf16[2560,1024]{1,0:T(8,128)(2,1)} %bitcast.5, bf16[2560,1024]{1,0:T(8,128)(2,1)} %bitcast.6, bf16[1024,2560]{1,0:T(8,128)(2,1)} %bitcast.7), custom_call_target="tpu_custom_call" | custom-call | tf_op jit(solution)/shard_map/pallas_call | solution.py:497
  133.5 2.0 %copy.8 = bf16[128,2560]{1,0:T(8,128)(2,1)} copy(bf16[128,2560]{1,0:T(8,128)(2,1)} %shard_map.64) | data formatting | bytes 1310720
